TPU v7x, 32 devices: a whole 2x2x4 slice. The times are simulated.
32 devices in a mesh: body: 16 (over z, x, core), row: 2 (over y).
Axes of the slice: x: 2, y: 2, z: 4, core: 2. Of those that a mesh axis runs over, the one named last changes fastest.
Arguments:
- strengths: bfloat16 [32, 131072], P(None, ('body', 'row')), may hold values from -6 to 6
- influence: bfloat16 [16, 2, 5, 32, 2, 128, 128], P('body', 'row'), may hold values from -0.09375 to 0.09375
- target_block: int32 [16, 2, 5, 32], P('body', 'row'), may hold values from 0 to 31
- source_block: int32 [16, 2, 5, 32], P('body', 'row'), may hold values from 0 to 63
- live_counts: int32 [16, 2, 5], P('body', 'row'), may hold values from 4 to 32, as said below
Outputs:
- response: float32 [32, 131072], P(None, ('body', 'row'))
Inputs may be any that keep to these rules, and one draw needn't show every extreme that they name: Slot k of a slice for source offset t is live when k < live_counts; for offset 2 (the group's own bodies) all 32 slots are live.
All inputs are finite; a program needn't handle non-finite values.
Results may differ from a plain program's by a relative error of at most 0.0003.
Values may be sent and summed in bfloat16 or wider, within the bound.
No kernel may reach another device: no remote copies, remote signals or barrier semaphores. Data moves between devices by JAX's collectives and lax.ppermute only.
A program may use at most 64 MiB of HBM per device.

v0:
```python
import functools

import jax
import jax.numpy as jnp
from jax import lax
from jax.experimental import pallas as pl
from jax.experimental.pallas import tpu as pltpu
from jax.sharding import PartitionSpec as P

AXES = ("body", "row")
UNROLL = 8
SMEM = pl.BlockSpec(memory_space=pltpu.SMEM)
VMEM = pl.BlockSpec(memory_space=pltpu.VMEM)


def send(array, move):
    bodies, rows = lax.axis_size("body"), lax.axis_size("row")
    pairs = []
    for body in range(bodies):
        for row in range(rows):
            to_body, to_row = move(body, row)
            pairs.append((body * rows + row, (to_body % bodies) * rows + to_row % rows))
    return lax.ppermute(array, AXES, pairs)


def prepare_kernel(route, stages, row_blocks, infl_ref, *refs):
    *small_refs, kept_ref, list_ref, tb_ref, sb_ref, live_ref, sems, small_sems = refs
    offsets, capacity = kept_ref.shape[:2]
    body, row = lax.axis_index("body"), lax.axis_index("row")
    last = list_ref.shape[1] - 1
    tb_copy, sb_copy, live_copy = (
        pltpu.make_async_copy(hbm, smem, small_sems.at[i])
        for i, (hbm, smem) in enumerate(zip(small_refs, (tb_ref, sb_ref, live_ref)))
    )
    live_copy.start()
    tb_copy.start()
    sb_copy.start()

    def tiles_copy(t, b):
        span = pl.ds(b * UNROLL, UNROLL)
        return pltpu.make_async_copy(infl_ref.at[0, 0, t, span], kept_ref.at[t, span], sems.at[t, b])

    def batches(t):
        return (live_ref[0, 0, t] + (UNROLL - 1)) // UNROLL

    for t in range(offsets):
        tiles_copy(t, 0).start()
    live_copy.wait()
    for t in range(offsets):
        lax.fori_loop(1, batches(t), lambda b, c, t=t: (tiles_copy(t, b).start(), c)[1], 0)
    tb_copy.wait()
    sb_copy.wait()

    counts = (jnp.int32(0),) * stages
    for t in range(offsets):
        live = live_ref[0, 0, t]
        ways = [route(body, row, t, s) for s in range(lax.axis_size("row"))]

        def batch(b, counts, t=t, live=live, ways=ways):
            counts = list(counts)
            for i in range(UNROLL):
                k = b * UNROLL + i
                sb = sb_ref[t, 0, k]
                stage, piece = ways[0]
                for s in range(1, len(ways)):
                    here = sb >= s * row_blocks
                    stage, piece = jnp.where(here, ways[s][0], stage), jnp.where(here, ways[s][1], piece)
                at = counts[0]
                for s in range(1, stages):
                    at = jnp.where(stage == s, counts[s], at)
                block = lax.rem(sb, row_blocks)
                list_ref[stage, at] = ((t * capacity + k) << 18) + ((piece * row_blocks + block) << 6) + tb_ref[t, 0, k]
                one = jnp.where(k < live, 1, 0)
                for s in range(stages):
                    counts[s] = counts[s] + jnp.where(stage == s, one, 0)
            return tuple(counts)

        counts = lax.fori_loop(0, batches(t), batch, counts)
    for s in range(stages):
        for i in range(UNROLL - 1):
            list_ref[s, counts[s] + i] = 0
        list_ref[s, last] = counts[s]
    for t in range(offsets):
        lax.fori_loop(0, batches(t), lambda b, c, t=t: (tiles_copy(t, b).wait(), c)[1], 0)


def prepare(influence, target_block, source_block, live_counts, route, stages, row_blocks):
    offsets, capacity = influence.shape[2:4]
    in_hbm = lambda a: pltpu.with_memory_space_constraint(a, pltpu.HBM)
    by_offset = lambda a: in_hbm(jnp.transpose(a, (0, 2, 1, 3)).reshape(offsets, 1, capacity))
    hbm = pl.BlockSpec(memory_space=pltpu.HBM)
    return pl.pallas_call(
        functools.partial(prepare_kernel, route, stages, row_blocks),
        out_shape=(
            jax.ShapeDtypeStruct(influence.shape[2:], influence.dtype),
            jax.ShapeDtypeStruct((stages, offsets * capacity + UNROLL), jnp.int32),
        ),
        in_specs=[hbm] * 4,
        out_specs=(pl.BlockSpec(memory_space=pl.ANY), SMEM),
        scratch_shapes=[
            pltpu.SMEM((offsets, 1, capacity), jnp.int32),
            pltpu.SMEM((offsets, 1, capacity), jnp.int32),
            pltpu.SMEM(live_counts.shape, jnp.int32),
            pltpu.SemaphoreType.DMA((offsets, capacity // UNROLL)),
            pltpu.SemaphoreType.DMA((3,)),
        ],
        compiler_params=pltpu.CompilerParams(vmem_limit_bytes=4 << 20),
        cost_estimate=pl.CostEstimate(flops=0, transcendentals=0, bytes_accessed=1024),
        name="prepare",
    )(in_hbm(influence), by_offset(target_block), by_offset(source_block), in_hbm(live_counts))


def slots_kernel(stage, *refs):
    *totals, src_ref, kept_ref, list_ref, out_ref = refs
    block_size, capacity = kept_ref.shape[-1], kept_ref.shape[1]
    piece_blocks = src_ref.shape[2] // block_size
    heads = src_ref.shape[1] // 2
    out_ref[...] = totals[0][...] if totals else 0.5 * src_ref[0].astype(jnp.float32)
    count = list_ref[stage, list_ref.shape[1] - 1]

    def compute(b, carry):
        products, columns = [], []
        for i in range(UNROLL):
            entry = list_ref[stage, b * UNROLL + i]
            slot, place, target = entry >> 18, (entry >> 6) & 4095, entry & 63
            column = pl.multiple_of((place % piece_blocks) * block_size, block_size)
            x = src_ref[place // piece_blocks, :, pl.ds(column, block_size)]
            x = jnp.where(b * UNROLL + i < count, x, jnp.zeros_like(x))
            turned = jnp.concatenate([-x[heads:], x[:heads]], axis=0)
            both = jnp.concatenate([x, turned], axis=1)
            t, k = slot // capacity, slot % capacity
            tiles = jnp.concatenate([kept_ref[t, k, 0], kept_ref[t, k, 1]], axis=1)
            products.append(lax.dot_general(both, tiles, (((1,), (1,)), ((), ())), preferred_element_type=jnp.float32))
            columns.append(pl.multiple_of(target * block_size, block_size))
        for product, column in zip(products, columns):
            out_ref[:, pl.ds(column, block_size)] += product
        return carry

    lax.fori_loop(0, (count + UNROLL - 1) // UNROLL, compute, 0)


def add_slots(totals, src, kept, lists, stage, name):
    return pl.pallas_call(
        functools.partial(slots_kernel, stage),
        out_shape=jax.ShapeDtypeStruct(src.shape[1:], jnp.float32),
        in_specs=[VMEM] * len(totals) + [VMEM, VMEM, SMEM],
        out_specs=VMEM,
        compiler_params=pltpu.CompilerParams(vmem_limit_bytes=4 << 20),
        cost_estimate=pl.CostEstimate(flops=0, transcendentals=0, bytes_accessed=1024),
        name=name,
    )(*totals, src, kept, lists)


EARLY, MIDDLE, LATE = range(3)


def chip_route(body, row, t, slot_slice):
    core, x = body % 2, (body // 2) % 2
    there = core + t - 2
    chip = (there + 2) // 2 - 1
    crossed = ((there + 2) % 2 != core).astype(jnp.int32)
    other_row = (slot_slice != row).astype(jnp.int32)
    own, near = chip == 0, chip == jnp.where(x == 0, 1, -1)
    both = crossed + other_row
    stage = jnp.where(own, both // 2, jnp.where(near, jnp.minimum(1 + both, LATE), both))
    own_piece = jnp.where(crossed == 0, other_row, 3 - other_row)
    near_piece = jnp.where(both == 0, 0, 2 * crossed - other_row * crossed)
    far_piece = jnp.where(both == 0, 2, jnp.where(both == 2, 3, 1 + 2 * crossed))
    piece = jnp.where(own, own_piece, jnp.where(near, near_piece, far_piece))
    return stage, piece


def across_x(body, row):
    return body ^ 2, row


def across_y(body, row):
    return body, 1 - row


def to_far_chip(body, row):
    return ((body ^ 2) + 4 if body & 2 else (body ^ 2) - 4), row


def other_core(body, row):
    return body ^ 1, row


def after(value, *earlier):
    return lax.optimization_barrier((value, *earlier))[0]


def both_cores(*pieces):
    mine = jnp.stack(pieces) if len(pieces) > 1 else pieces[0][None]
    return jnp.concatenate([mine, send(mine, other_core)])


def by_chips(x, influence, target_block, source_block, live_counts):
    row_blocks = x.shape[1] // influence.shape[-1]
    kept, lists = prepare(
        influence, target_block, source_block, live_counts, chip_route, 3, row_blocks
    )
    half = x.shape[1] // 2
    half = x.shape[1] // 2
    far = send(x, to_far_chip)
    near = send(x, across_x)
    own_other = send(x, across_y)
    crossed_x = send(x, other_core)
    far, own_other, kept, lists = lax.optimization_barrier((far, own_other, kept, lists))
    far_other = send(far, across_y)
    near_other = send(own_other, across_x)
    crossed = [send(piece, other_core) for piece in (own_other, far)]
    total = add_slots([], jnp.stack([x, own_other, far, crossed_x]), kept, lists, EARLY, "early_slots")
    middle = jnp.stack([after(near, total), far_other, *crossed])
    crossed = [send(piece, other_core) for piece in (near, far_other)]
    total = add_slots([total], middle, kept, lists, MIDDLE, "middle_slots")
    near_other = after(near_other, total, *crossed)
    late = jnp.stack([near_other, send(near_other, other_core), *crossed])
    return add_slots([total], late, kept, lists, LATE, "late_slots")


def plain_route(rows, body, row, t, slot_slice):
    return 0, 1 + t * rows + slot_slice


def plain(x, influence, target_block, source_block, live_counts):
    rows, reach = lax.axis_size("row"), (influence.shape[2] - 1) // 2
    row_blocks = x.shape[1] // influence.shape[-1]
    route = functools.partial(plain_route, rows)
    kept, lists = prepare(influence, target_block, source_block, live_counts, route, 1, row_blocks)
    group = jnp.moveaxis(lax.all_gather(x, "row", axis=1, tiled=True).reshape(x.shape[0], rows, -1), 1, 0)
    shifted = lambda by: send(group, lambda body, row: (body - by, row))
    src = jnp.concatenate([x[None]] + [shifted(by) if by else group for by in range(-reach, reach + 1)])
    return add_slots([], src, kept, lists, 0, "slots")


def on_device(strengths, influence, target_block, source_block, live_counts):
    bodies, rows = lax.axis_size("body"), lax.axis_size("row")
    on_chips = rows == 2 and influence.shape[2] == 5 and bodies % 4 == 0 and bodies >= 8
    return (by_chips if on_chips else plain)(strengths, influence, target_block, source_block, live_counts)


def solution(mesh):
    return jax.shard_map(
        on_device,
        mesh=mesh,
        in_specs=(
            P(None, ("body", "row")),
            P("body", "row", None, None, None, None, None),
            P("body", "row", None, None),
            P("body", "row", None, None),
            P("body", "row", None),
        ),
        out_specs=P(None, ("body", "row")),
        check_vma=False,
    )
```

profile of v0, /device:TPU:0, one launch (start us, length us, event | category | flops | bytes accessed | tf_op | source)
XLA Modules:
  0.0 28.2 jit_solution(4157661724077301682)
XLA Ops:
  0.0 0.0 copy-start
  0.0 6.0 %collective-permute-start = (bf16[32,4096]{1,0:T(8,128)(2,1)}, bf16[32,4096]{1,0:T(8,128)(2,1)S(1)}, u32[]{:S(2)}, u32[]{:S(2)}) collective-permute-start(bf16[32,4096]{1,0:T(8,128)(2,1)} %param.5), channel_id=1, source_target_pairs={{0,28},{1,29},{2,30},{3,31},{4,8},{5,9},{6,10},{7,11},{8,4},{9,5},... | collective-permute-start | bytes 786440 | tf_op jit(solution)/shard_map/ppermute | solution.py:23
  6.0 1.5 %collective-permute-start.1 = (bf16[32,4096]{1,0:T(8,128)(2,1)}, bf16[32,4096]{1,0:T(8,128)(2,1)S(1)}, u32[]{:S(2)}, u32[]{:S(2)}) collective-permute-start(bf16[32,4096]{1,0:T(8,128)(2,1)} %param.5), channel_id=1, source_target_pairs={{0,1},{1,0},{2,3},{3,2},{4,5},{5,4},{6,7},{7,6},{8,9},{9,8},{10,11... | collective-permute-start | bytes 786440 | tf_op jit(solution)/shard_map/ppermute | solution.py:23
  7.5 0.0 collective-permute-start.2
  7.5 0.0 collective-permute-start.3
  7.5 4.1 %prepare.1 = (bf16[5,32,2,128,128]{4,3,2,1,0:T(8,128)(2,1)S(1)}, s32[3,168]{1,0:T(4,128)S(1)}) custom-call(bf16[1,1,5,32,2,128,128]{6,5,4,3,2,1,0:T(8,128)(2,1)} %infl_ref.1, s32[5,1,32]{2,1,0:T(1,128)} %bitcast.26, s32[5,1,32]{2,1,0:T(1,128)} %bitcast.27, s32[1,1,5]{2,1,0:T(1,128)} %refs_2_.1), custom_call_target="tpu_custom_call" | custom-call | bytes 1024 | tf_op jit(solution)/shard_map/prepare/pallas_call | solution.py:92
  11.6 1.0 %collective-permute-done = bf16[32,4096]{1,0:T(8,128)(2,1)S(1)} collective-permute-done((bf16[32,4096]{1,0:T(8,128)(2,1)}, bf16[32,4096]{1,0:T(8,128)(2,1)S(1)}, u32[]{:S(2)}, u32[]{:S(2)}) %collective-permute-start) | collective-permute-done | bytes 262176 | tf_op jit(solution)/shard_map/ppermute | solution.py:23
  12.7 1.3 %collective-permute-done.1 = bf16[32,4096]{1,0:T(8,128)(2,1)S(1)} collective-permute-done((bf16[32,4096]{1,0:T(8,128)(2,1)}, bf16[32,4096]{1,0:T(8,128)(2,1)S(1)}, u32[]{:S(2)}, u32[]{:S(2)}) %collective-permute-start.1) | collective-permute-done | bytes 262176 | tf_op jit(solution)/shard_map/ppermute | solution.py:23
  14.0 1.5 %collective-permute-start.4 = (bf16[32,4096]{1,0:T(8,128)(2,1)S(1)}, bf16[32,4096]{1,0:T(8,128)(2,1)S(1)}, u32[]{:S(2)}, u32[]{:S(2)}) collective-permute-start(bf16[32,4096]{1,0:T(8,128)(2,1)S(1)} %collective-permute-done), channel_id=1, source_target_pairs={{0,1},{1,0},{2,3},{3,2},{4,5},{5,4},{6,7},{7,6},{8,9},{9,8},{10,11... | collective-permute-start | bytes 786440 | tf_op jit(solution)/shard_map/ppermute | solution.py:23
  15.5 0.0 collective-permute-start.6
  15.5 0.5 %collective-permute-start.5 = (bf16[32,4096]{1,0:T(8,128)(2,1)S(1)}, bf16[32,4096]{1,0:T(8,128)(2,1)S(1)}, u32[]{:S(2)}, u32[]{:S(2)}) collective-permute-start(bf16[32,4096]{1,0:T(8,128)(2,1)S(1)} %collective-permute-done.1), channel_id=1, source_target_pairs={{0,2},{1,3},{2,0},{3,1},{4,6},{5,7},{6,4},{7,5},{8,10},{9,11},{10,... | collective-permute-start | bytes 786440 | tf_op jit(solution)/shard_map/ppermute | solution.py:23
  16.0 0.0 collective-permute-done.2
  16.0 0.0 collective-permute-start.7
  16.0 0.0 copy-done
  16.0 0.1 pad_maximum_fusion.refs_0_
  16.1 2.4 %early_slots.1.refs_0_ = f32[32,4096]{1,0:T(8,128)S(1)} custom-call(bf16[4,32,4096]{2,1,0:T(8,128)(2,1)S(1)} %pad_maximum_fusion.refs_0_, bf16[5,32,2,128,128]{4,3,2,1,0:T(8,128)(2,1)S(1)} %get-tuple-element.17.refs_1_.refs_2_, s32[3,168]{1,0:T(4,128)S(1)} %get-tuple-element.18.refs_2_.refs_3_), custom_call_target="tpu_custom_call" | custom-call | bytes 1024 | tf_op jit(solution)/shard_map/early_slots/pallas_call | solution.py:143
  18.5 0.0 collective-permute-done.3
  18.5 0.1 collective-permute-start.8
  18.6 2.2 %collective-permute-done.4 = bf16[32,4096]{1,0:T(8,128)(2,1)S(1)} collective-permute-done((bf16[32,4096]{1,0:T(8,128)(2,1)S(1)}, bf16[32,4096]{1,0:T(8,128)(2,1)S(1)}, u32[]{:S(2)}, u32[]{:S(2)}) %collective-permute-start.4) | collective-permute-done | bytes 262176 | tf_op jit(solution)/shard_map/ppermute | solution.py:23
  20.8 0.0 collective-permute-start.9
  20.8 0.0 collective-permute-done.5
  20.8 0.0 collective-permute-done.6
  20.8 0.1 pad_maximum_fusion.1.refs_1_
  21.0 2.3 %middle_slots.1.refs_0_ = f32[32,4096]{1,0:T(8,128)S(1)} custom-call(f32[32,4096]{1,0:T(8,128)S(1)} %early_slots.1.refs_0_, bf16[4,32,4096]{2,1,0:T(8,128)(2,1)S(1)} %pad_maximum_fusion.1.refs_1_, bf16[5,32,2,128,128]{4,3,2,1,0:T(8,128)(2,1)S(1)} %get-tuple-element.17.refs_1_.refs_2_, s32[3,168]{1,0:T(4,128)S(1)} %get-tuple-element.18.refs_2_.refs_3_), custom_call_target="tpu_custom_call" | custom-call | bytes 1024 | tf_op jit(solution)/shard_map/middle_slots/pallas_call | solution.py:143
  23.3 0.9 %collective-permute-done.7 = bf16[32,4096]{1,0:T(8,128)(2,1)S(1)} collective-permute-done((bf16[32,4096]{1,0:T(8,128)(2,1)S(1)}, bf16[32,4096]{1,0:T(8,128)(2,1)S(1)}, u32[]{:S(2)}, u32[]{:S(2)}) %collective-permute-start.7) | collective-permute-done | bytes 262176 | tf_op jit(solution)/shard_map/ppermute | solution.py:23
  24.2 0.0 collective-permute-done.8
  24.2 0.0 collective-permute-done.9
  24.2 0.0 collective-permute-start.10
  24.2 1.5 %collective-permute-done.10 = bf16[32,4096]{1,0:T(8,128)(2,1)S(1)} collective-permute-done((bf16[32,4096]{1,0:T(8,128)(2,1)S(1)}, bf16[32,4096]{1,0:T(8,128)(2,1)S(1)}, u32[]{:S(2)}, u32[]{:S(2)}) %collective-permute-start.10) | collective-permute-done | bytes 262176 | tf_op jit(solution)/shard_map/ppermute | solution.py:23
  25.8 0.1 pad_maximum_fusion.2.refs_1_
  25.9 2.3 %late_slots.1 = f32[32,4096]{1,0:T(8,128)} custom-call(f32[32,4096]{1,0:T(8,128)S(1)} %middle_slots.1.refs_0_, bf16[4,32,4096]{2,1,0:T(8,128)(2,1)S(1)} %pad_maximum_fusion.2.refs_1_, bf16[5,32,2,128,128]{4,3,2,1,0:T(8,128)(2,1)S(1)} %get-tuple-element.17.refs_1_.refs_2_, s32[3,168]{1,0:T(4,128)S(1)} %get-tuple-element.18.refs_2_.refs_3_), custom_call_target="tpu_custom_call" | custom-call | bytes 1024 | tf_op jit(solution)/shard_map/late_slots/pallas_call | solution.py:143
Async XLA Ops:
  0.0 16.0 %copy-start = (bf16[32,4096]{1,0:T(8,128)(2,1)S(1)}, bf16[32,4096]{1,0:T(8,128)(2,1)}, u32[]{:S(2)}) copy-start(bf16[32,4096]{1,0:T(8,128)(2,1)} %param.5) | copy-start | bytes 786436
  0.0 12.7 %collective-permute-start = (bf16[32,4096]{1,0:T(8,128)(2,1)}, bf16[32,4096]{1,0:T(8,128)(2,1)S(1)}, u32[]{:S(2)}, u32[]{:S(2)}) collective-permute-start(bf16[32,4096]{1,0:T(8,128)(2,1)} %param.5), channel_id=1, source_target_pairs={{0,28},{1,29},{2,30},{3,31},{4,8},{5,9},{6,10},{7,11},{8,4},{9,5},... | collective-permute-start | bytes 786440 | tf_op jit(solution)/shard_map/ppermute | solution.py:23
  6.0 8.0 %collective-permute-start.1 = (bf16[32,4096]{1,0:T(8,128)(2,1)}, bf16[32,4096]{1,0:T(8,128)(2,1)S(1)}, u32[]{:S(2)}, u32[]{:S(2)}) collective-permute-start(bf16[32,4096]{1,0:T(8,128)(2,1)} %param.5), channel_id=1, source_target_pairs={{0,1},{1,0},{2,3},{3,2},{4,5},{5,4},{6,7},{7,6},{8,9},{9,8},{10,11... | collective-permute-start | bytes 786440 | tf_op jit(solution)/shard_map/ppermute | solution.py:23
  7.5 8.5 %collective-permute-start.2 = (bf16[32,4096]{1,0:T(8,128)(2,1)}, bf16[32,4096]{1,0:T(8,128)(2,1)S(1)}, u32[]{:S(2)}, u32[]{:S(2)}) collective-permute-start(bf16[32,4096]{1,0:T(8,128)(2,1)} %param.5), channel_id=1, source_target_pairs={{0,2},{1,3},{2,0},{3,1},{4,6},{5,7},{6,4},{7,5},{8,10},{9,11},{10,... | collective-permute-start | bytes 786440 | tf_op jit(solution)/shard_map/ppermute | solution.py:23
  7.5 11.0 %collective-permute-start.3 = (bf16[32,4096]{1,0:T(8,128)(2,1)}, bf16[32,4096]{1,0:T(8,128)(2,1)S(1)}, u32[]{:S(2)}, u32[]{:S(2)}) collective-permute-start(bf16[32,4096]{1,0:T(8,128)(2,1)} %param.5), channel_id=1, source_target_pairs={{0,4},{1,5},{2,6},{3,7},{4,0},{5,1},{6,2},{7,3},{8,12},{9,13},{10,... | collective-permute-start | bytes 786440 | tf_op jit(solution)/shard_map/ppermute | solution.py:23
  14.0 6.9 %collective-permute-start.4 = (bf16[32,4096]{1,0:T(8,128)(2,1)S(1)}, bf16[32,4096]{1,0:T(8,128)(2,1)S(1)}, u32[]{:S(2)}, u32[]{:S(2)}) collective-permute-start(bf16[32,4096]{1,0:T(8,128)(2,1)S(1)} %collective-permute-done), channel_id=1, source_target_pairs={{0,1},{1,0},{2,3},{3,2},{4,5},{5,4},{6,7},{7,6},{8,9},{9,8},{10,11... | collective-permute-start | bytes 786440 | tf_op jit(solution)/shard_map/ppermute | solution.py:23
  15.5 5.3 %collective-permute-start.6 = (bf16[32,4096]{1,0:T(8,128)(2,1)S(1)}, bf16[32,4096]{1,0:T(8,128)(2,1)S(1)}, u32[]{:S(2)}, u32[]{:S(2)}) collective-permute-start(bf16[32,4096]{1,0:T(8,128)(2,1)S(1)} %collective-permute-done), channel_id=1, source_target_pairs={{0,2},{1,3},{2,0},{3,1},{4,6},{5,7},{6,4},{7,5},{8,10},{9,11},{10,... | collective-permute-start | bytes 786440 | tf_op jit(solution)/shard_map/ppermute | solution.py:23
  15.5 5.3 %collective-permute-start.5 = (bf16[32,4096]{1,0:T(8,128)(2,1)S(1)}, bf16[32,4096]{1,0:T(8,128)(2,1)S(1)}, u32[]{:S(2)}, u32[]{:S(2)}) collective-permute-start(bf16[32,4096]{1,0:T(8,128)(2,1)S(1)} %collective-permute-done.1), channel_id=1, source_target_pairs={{0,2},{1,3},{2,0},{3,1},{4,6},{5,7},{6,4},{7,5},{8,10},{9,11},{10,... | collective-permute-start | bytes 786440 | tf_op jit(solution)/shard_map/ppermute | solution.py:23
  16.0 8.2 %collective-permute-start.7 = (bf16[32,4096]{1,0:T(8,128)(2,1)S(1)}, bf16[32,4096]{1,0:T(8,128)(2,1)S(1)}, u32[]{:S(2)}, u32[]{:S(2)}) collective-permute-start(bf16[32,4096]{1,0:T(8,128)(2,1)S(1)} %collective-permute-done.1), channel_id=1, source_target_pairs={{0,4},{1,5},{2,6},{3,7},{4,0},{5,1},{6,2},{7,3},{8,12},{9,13},{10,... | collective-permute-start | bytes 786440 | tf_op jit(solution)/shard_map/ppermute | solution.py:23
  18.5 5.7 %collective-permute-start.8 = (bf16[32,4096]{1,0:T(8,128)(2,1)S(1)}, bf16[32,4096]{1,0:T(8,128)(2,1)S(1)}, u32[]{:S(2)}, u32[]{:S(2)}) collective-permute-start(bf16[32,4096]{1,0:T(8,128)(2,1)S(1)} %collective-permute-done.3), channel_id=1, source_target_pairs={{0,2},{1,3},{2,0},{3,1},{4,6},{5,7},{6,4},{7,5},{8,10},{9,11},{10,... | collective-permute-start | bytes 786440 | tf_op jit(solution)/shard_map/ppermute | solution.py:23
  20.8 3.4 %collective-permute-start.9 = (bf16[32,4096]{1,0:T(8,128)(2,1)S(1)}, bf16[32,4096]{1,0:T(8,128)(2,1)S(1)}, u32[]{:S(2)}, u32[]{:S(2)}) collective-permute-start(bf16[32,4096]{1,0:T(8,128)(2,1)S(1)} %collective-permute-done.4), channel_id=1, source_target_pairs={{0,2},{1,3},{2,0},{3,1},{4,6},{5,7},{6,4},{7,5},{8,10},{9,11},{10,... | collective-permute-start | bytes 786440 | tf_op jit(solution)/shard_map/ppermute | solution.py:23
  24.2 1.5 %collective-permute-start.10 = (bf16[32,4096]{1,0:T(8,128)(2,1)S(1)}, bf16[32,4096]{1,0:T(8,128)(2,1)S(1)}, u32[]{:S(2)}, u32[]{:S(2)}) collective-permute-start(bf16[32,4096]{1,0:T(8,128)(2,1)S(1)} %collective-permute-done.7), channel_id=1, source_target_pairs={{0,2},{1,3},{2,0},{3,1},{4,6},{5,7},{6,4},{7,5},{8,10},{9,11},{10,... | collective-permute-start | bytes 786440 | tf_op jit(solution)/shard_map/ppermute | solution.py:23
where the time goes:
time: 28.3 us; the launch traced here: 28.2 us
  Pallas kernels  11.1 us (39%)
  starting transfers between devices  9.61 us (34%)
  waiting for transfers between devices  6.96 us (25%)
  other arithmetic  0.4 us (1%)
    ppermute x11, starting transfers between devices, send(): return lax.ppermute(array, AXES, pairs)  9.61 us
    pallas_call x3, Pallas kernels, add_slots(): pl.pallas_call(functools.partial(slots_kernel, stage), out_shape=jax.Shap...  6.99 us
    ppermute x11, waiting for transfers between devices, send(): return lax.ppermute(array, AXES, pairs)  6.96 us
    pallas_call x1, Pallas kernels, prepare(): pl.pallas_call(functools.partial(prepare_kernel, route, stages, row_block...  4.13 us
  transfers between devices with their start and end apart: 11, of which 5 were waited for; matrix products, arithmetic and copies ran while one was open for 1% of the time, Pallas kernels for 31%

commit v1 on v0

--- a/solution.py
+++ b/solution.py
@@ -61,15 +61,15 @@
             for i in range(UNROLL):
                 k = b * UNROLL + i
                 sb = sb_ref[t, 0, k]
-                stage, piece = ways[0]
+                block, (stage, piece) = sb, ways[0]
                 for s in range(1, len(ways)):
                     here = sb >= s * row_blocks
+                    block = jnp.where(here, sb - s * row_blocks, block)
                     stage, piece = jnp.where(here, ways[s][0], stage), jnp.where(here, ways[s][1], piece)
                 at = counts[0]
                 for s in range(1, stages):
                     at = jnp.where(stage == s, counts[s], at)
-                block = lax.rem(sb, row_blocks)
-                list_ref[stage, at] = ((t * capacity + k) << 18) + ((piece * row_blocks + block) << 6) + tb_ref[t, 0, k]
+                list_ref[stage, at] = ((t * capacity + k) << 18) + (piece << 12) + (block << 6) + tb_ref[t, 0, k]
                 one = jnp.where(k < live, 1, 0)
                 for s in range(stages):
                     counts[s] = counts[s] + jnp.where(stage == s, one, 0)
@@ -112,8 +112,8 @@
 
 def slots_kernel(stage, *refs):
     *totals, src_ref, kept_ref, list_ref, out_ref = refs
-    block_size, capacity = kept_ref.shape[-1], kept_ref.shape[1]
-    piece_blocks = src_ref.shape[2] // block_size
+    last_ref = totals.pop() if len(totals) > 1 else None
+    block_size = kept_ref.shape[-1]
     heads = src_ref.shape[1] // 2
     out_ref[...] = totals[0][...] if totals else 0.5 * src_ref[0].astype(jnp.float32)
     count = list_ref[stage, list_ref.shape[1] - 1]
@@ -122,14 +122,17 @@
         products, columns = [], []
         for i in range(UNROLL):
             entry = list_ref[stage, b * UNROLL + i]
-            slot, place, target = entry >> 18, (entry >> 6) & 4095, entry & 63
-            column = pl.multiple_of((place % piece_blocks) * block_size, block_size)
-            x = src_ref[place // piece_blocks, :, pl.ds(column, block_size)]
+            slot, piece, block, target = entry >> 18, (entry >> 12) & 63, (entry >> 6) & 63, entry & 63
+            column = pl.multiple_of(block * block_size, block_size)
+            if last_ref is None:
+                x = src_ref[piece, :, pl.ds(column, block_size)]
+            else:
+                x = src_ref[jnp.minimum(piece, src_ref.shape[0] - 1), :, pl.ds(column, block_size)]
+                x = jnp.where(piece < src_ref.shape[0], x, last_ref[:, pl.ds(column, block_size)])
             x = jnp.where(b * UNROLL + i < count, x, jnp.zeros_like(x))
             turned = jnp.concatenate([-x[heads:], x[:heads]], axis=0)
             both = jnp.concatenate([x, turned], axis=1)
-            t, k = slot // capacity, slot % capacity
-            tiles = jnp.concatenate([kept_ref[t, k, 0], kept_ref[t, k, 1]], axis=1)
+            tiles = jnp.concatenate([kept_ref[slot, 0], kept_ref[slot, 1]], axis=1)
             products.append(lax.dot_general(both, tiles, (((1,), (1,)), ((), ())), preferred_element_type=jnp.float32))
             columns.append(pl.multiple_of(target * block_size, block_size))
         for product, column in zip(products, columns):
@@ -148,7 +151,7 @@
         compiler_params=pltpu.CompilerParams(vmem_limit_bytes=4 << 20),
         cost_estimate=pl.CostEstimate(flops=0, transcendentals=0, bytes_accessed=1024),
         name=name,
-    )(*totals, src, kept, lists)
+    )(*totals, src, kept.reshape((-1,) + kept.shape[2:]), lists)
 
 
 EARLY, MIDDLE, LATE = range(3)
@@ -164,8 +167,8 @@
     both = crossed + other_row
     stage = jnp.where(own, both // 2, jnp.where(near, jnp.minimum(1 + both, LATE), both))
     own_piece = jnp.where(crossed == 0, other_row, 3 - other_row)
-    near_piece = jnp.where(both == 0, 0, 2 * crossed - other_row * crossed)
-    far_piece = jnp.where(both == 0, 2, jnp.where(both == 2, 3, 1 + 2 * crossed))
+    near_piece = crossed * (1 + 2 * other_row)
+    far_piece = jnp.where(both == 1, 1 + 2 * crossed, 2)
     piece = jnp.where(own, own_piece, jnp.where(near, near_piece, far_piece))
     return stage, piece
 
@@ -200,8 +203,6 @@
     kept, lists = prepare(
         influence, target_block, source_block, live_counts, chip_route, 3, row_blocks
     )
-    half = x.shape[1] // 2
-    half = x.shape[1] // 2
     far = send(x, to_far_chip)
     near = send(x, across_x)
     own_other = send(x, across_y)
@@ -215,8 +216,8 @@
     crossed = [send(piece, other_core) for piece in (near, far_other)]
     total = add_slots([total], middle, kept, lists, MIDDLE, "middle_slots")
     near_other = after(near_other, total, *crossed)
-    late = jnp.stack([near_other, send(near_other, other_core), *crossed])
-    return add_slots([total], late, kept, lists, LATE, "late_slots")
+    late = jnp.stack([near_other, *crossed])
+    return add_slots([total, send(near_other, other_core)], late, kept, lists, LATE, "late_slots")
 
 
 def plain_route(rows, body, row, t, slot_slice):

time: 28.3 us -> 27.9 us (0.986)
  waiting for transfers between devices: 6.96 us -> 6.39 us
  Pallas kernels: 11.1 us -> 11.6 us
    ppermute x11, waiting for transfers between devices: 6.96 us -> 6.39 us  [send(): return lax.ppermute(array, AXES, pairs)]
    pallas_call x3, Pallas kernels: 6.99 us -> 7.33 us  [add_slots(): pl.pallas_call(functools.partial(slots_kernel, stage), out_shape=jax.Shap...]
  transfers between devices with their start and end apart: 11 -> 11, of which waited for: 5 -> 5; matrix products, arithmetic and copies ran while one was open for 1% -> 1% of each run, Pallas kernels for 31% -> 33%
where the time goes in v1:
time: 27.9 us; the launch traced here: 28.1 us
  Pallas kernels  11.6 us (42%)
  starting transfers between devices  9.61 us (34%)
  waiting for transfers between devices  6.39 us (23%)
  other arithmetic  0.36 us (1%)
    ppermute x11, starting transfers between devices, send(): return lax.ppermute(array, AXES, pairs)  9.61 us
    pallas_call x3, Pallas kernels, add_slots(): pl.pallas_call(functools.partial(slots_kernel, stage), out_shape=jax.Shap...  7.33 us
    ppermute x11, waiting for transfers between devices, send(): return lax.ppermute(array, AXES, pairs)  6.39 us
    pallas_call x1, Pallas kernels, prepare(): pl.pallas_call(functools.partial(prepare_kernel, route, stages, row_block...  4.28 us
  transfers between devices with their start and end apart: 11, of which 5 were waited for; matrix products, arithmetic and copies ran while one was open for 1% of the time, Pallas kernels for 33%

profile of v1, /device:TPU:0, one launch (start us, length us, event | category | flops | bytes accessed | tf_op | source)
XLA Modules:
  0.0 28.1 jit_solution(10776653839253620000)
XLA Ops:
  0.0 0.0 copy-start
  0.0 6.0 %collective-permute-start = (bf16[32,4096]{1,0:T(8,128)(2,1)}, bf16[32,4096]{1,0:T(8,128)(2,1)S(1)}, u32[]{:S(2)}, u32[]{:S(2)}) collective-permute-start(bf16[32,4096]{1,0:T(8,128)(2,1)} %param.5), channel_id=1, source_target_pairs={{0,28},{1,29},{2,30},{3,31},{4,8},{5,9},{6,10},{7,11},{8,4},{9,5},... | collective-permute-start | bytes 786440 | tf_op jit(solution)/shard_map/ppermute | solution.py:23
  6.0 1.5 %collective-permute-start.1 = (bf16[32,4096]{1,0:T(8,128)(2,1)}, bf16[32,4096]{1,0:T(8,128)(2,1)S(1)}, u32[]{:S(2)}, u32[]{:S(2)}) collective-permute-start(bf16[32,4096]{1,0:T(8,128)(2,1)} %param.5), channel_id=1, source_target_pairs={{0,1},{1,0},{2,3},{3,2},{4,5},{5,4},{6,7},{7,6},{8,9},{9,8},{10,11... | collective-permute-start | bytes 786440 | tf_op jit(solution)/shard_map/ppermute | solution.py:23
  7.5 0.0 collective-permute-start.2
  7.5 0.0 collective-permute-start.3
  7.5 4.3 %prepare.1 = (bf16[5,32,2,128,128]{4,3,2,1,0:T(8,128)(2,1)S(1)}, s32[3,168]{1,0:T(4,128)S(1)}) custom-call(bf16[1,1,5,32,2,128,128]{6,5,4,3,2,1,0:T(8,128)(2,1)} %infl_ref.1, s32[5,1,32]{2,1,0:T(1,128)} %bitcast.28, s32[5,1,32]{2,1,0:T(1,128)} %bitcast.29, s32[1,1,5]{2,1,0:T(1,128)} %refs_2_.1), custom_call_target="tpu_custom_call" | custom-call | bytes 1024 | tf_op jit(solution)/shard_map/prepare/pallas_call | solution.py:92
  11.8 0.9 %collective-permute-done = bf16[32,4096]{1,0:T(8,128)(2,1)S(1)} collective-permute-done((bf16[32,4096]{1,0:T(8,128)(2,1)}, bf16[32,4096]{1,0:T(8,128)(2,1)S(1)}, u32[]{:S(2)}, u32[]{:S(2)}) %collective-permute-start) | collective-permute-done | bytes 262176 | tf_op jit(solution)/shard_map/ppermute | solution.py:23
  12.7 1.3 %collective-permute-done.1 = bf16[32,4096]{1,0:T(8,128)(2,1)S(1)} collective-permute-done((bf16[32,4096]{1,0:T(8,128)(2,1)}, bf16[32,4096]{1,0:T(8,128)(2,1)S(1)}, u32[]{:S(2)}, u32[]{:S(2)}) %collective-permute-start.1) | collective-permute-done | bytes 262176 | tf_op jit(solution)/shard_map/ppermute | solution.py:23
  14.0 1.5 %collective-permute-start.4 = (bf16[32,4096]{1,0:T(8,128)(2,1)S(1)}, bf16[32,4096]{1,0:T(8,128)(2,1)S(1)}, u32[]{:S(2)}, u32[]{:S(2)}) collective-permute-start(bf16[32,4096]{1,0:T(8,128)(2,1)S(1)} %collective-permute-done), channel_id=1, source_target_pairs={{0,1},{1,0},{2,3},{3,2},{4,5},{5,4},{6,7},{7,6},{8,9},{9,8},{10,11... | collective-permute-start | bytes 786440 | tf_op jit(solution)/shard_map/ppermute | solution.py:23
  15.5 0.0 collective-permute-start.6
  15.5 0.5 %collective-permute-start.5 = (bf16[32,4096]{1,0:T(8,128)(2,1)S(1)}, bf16[32,4096]{1,0:T(8,128)(2,1)S(1)}, u32[]{:S(2)}, u32[]{:S(2)}) collective-permute-start(bf16[32,4096]{1,0:T(8,128)(2,1)S(1)} %collective-permute-done.1), channel_id=1, source_target_pairs={{0,2},{1,3},{2,0},{3,1},{4,6},{5,7},{6,4},{7,5},{8,10},{9,11},{10,... | collective-permute-start | bytes 786440 | tf_op jit(solution)/shard_map/ppermute | solution.py:23
  16.0 0.0 collective-permute-done.2
  16.0 0.0 collective-permute-start.7
  16.0 0.0 copy-done
  16.0 0.1 pad_maximum_fusion.refs_0_
  16.1 2.9 %early_slots.1.refs_0_ = f32[32,4096]{1,0:T(8,128)S(1)} custom-call(bf16[4,32,4096]{2,1,0:T(8,128)(2,1)S(1)} %pad_maximum_fusion.refs_0_, bf16[160,2,128,128]{3,2,1,0:T(8,128)(2,1)S(1)} %bitcast.14, s32[3,168]{1,0:T(4,128)S(1)} %get-tuple-element.18.refs_2_.refs_3_.refs_4_), custom_call_target="tpu_custom_call" | custom-call | bytes 1024 | tf_op jit(solution)/shard_map/early_slots/pallas_call | solution.py:146
  19.1 0.0 collective-permute-done.3
  19.1 0.1 collective-permute-start.8
  19.2 1.6 %collective-permute-done.4 = bf16[32,4096]{1,0:T(8,128)(2,1)S(1)} collective-permute-done((bf16[32,4096]{1,0:T(8,128)(2,1)S(1)}, bf16[32,4096]{1,0:T(8,128)(2,1)S(1)}, u32[]{:S(2)}, u32[]{:S(2)}) %collective-permute-start.4) | collective-permute-done | bytes 262176 | tf_op jit(solution)/shard_map/ppermute | solution.py:23
  20.8 0.0 collective-permute-start.9
  20.8 0.0 collective-permute-done.6
  20.8 0.0 collective-permute-done.5
  20.8 0.1 pad_maximum_fusion.1.refs_1_
  21.0 2.1 %middle_slots.1.refs_0_ = f32[32,4096]{1,0:T(8,128)S(1)} custom-call(f32[32,4096]{1,0:T(8,128)S(1)} %early_slots.1.refs_0_, bf16[4,32,4096]{2,1,0:T(8,128)(2,1)S(1)} %pad_maximum_fusion.1.refs_1_, bf16[160,2,128,128]{3,2,1,0:T(8,128)(2,1)S(1)} %bitcast.15, s32[3,168]{1,0:T(4,128)S(1)} %get-tuple-element.18.refs_2_.refs_3_.refs_4_), custom_call_target="tpu_custom_call" | custom-call | bytes 1024 | tf_op jit(solution)/shard_map/middle_slots/pallas_call | solution.py:146
  23.1 1.2 %collective-permute-done.7 = bf16[32,4096]{1,0:T(8,128)(2,1)S(1)} collective-permute-done((bf16[32,4096]{1,0:T(8,128)(2,1)S(1)}, bf16[32,4096]{1,0:T(8,128)(2,1)S(1)}, u32[]{:S(2)}, u32[]{:S(2)}) %collective-permute-start.7) | collective-permute-done | bytes 262176 | tf_op jit(solution)/shard_map/ppermute | solution.py:23
  24.2 0.0 collective-permute-done.8
  24.2 0.0 collective-permute-done.9
  24.2 0.0 collective-permute-start.10
  24.2 0.1 pad_maximum_fusion.2.refs_2_
  24.3 1.4 %collective-permute-done.10.refs_1_ = bf16[32,4096]{1,0:T(8,128)(2,1)S(1)} collective-permute-done((bf16[32,4096]{1,0:T(8,128)(2,1)S(1)}, bf16[32,4096]{1,0:T(8,128)(2,1)S(1)}, u32[]{:S(2)}, u32[]{:S(2)}) %collective-permute-start.10) | collective-permute-done | bytes 262176 | tf_op jit(solution)/shard_map/ppermute | solution.py:23
  25.8 2.3 %late_slots.1 = f32[32,4096]{1,0:T(8,128)} custom-call(f32[32,4096]{1,0:T(8,128)S(1)} %middle_slots.1.refs_0_, bf16[32,4096]{1,0:T(8,128)(2,1)S(1)} %collective-permute-done.10.refs_1_, bf16[3,32,4096]{2,1,0:T(8,128)(2,1)S(1)} %pad_maximum_fusion.2.refs_2_, bf16[160,2,128,128]{3,2,1,0:T(8,128)(2,1)S(1)} %bitcast.16, ...), custom_call_target="tpu_custom_call" | custom-call | bytes 1024 | tf_op jit(solution)/shard_map/late_slots/pallas_call | solution.py:146
Async XLA Ops:
  0.0 16.0 %copy-start = (bf16[32,4096]{1,0:T(8,128)(2,1)S(1)}, bf16[32,4096]{1,0:T(8,128)(2,1)}, u32[]{:S(2)}) copy-start(bf16[32,4096]{1,0:T(8,128)(2,1)} %param.5) | copy-start | bytes 786436
  0.0 12.7 %collective-permute-start = (bf16[32,4096]{1,0:T(8,128)(2,1)}, bf16[32,4096]{1,0:T(8,128)(2,1)S(1)}, u32[]{:S(2)}, u32[]{:S(2)}) collective-permute-start(bf16[32,4096]{1,0:T(8,128)(2,1)} %param.5), channel_id=1, source_target_pairs={{0,28},{1,29},{2,30},{3,31},{4,8},{5,9},{6,10},{7,11},{8,4},{9,5},... | collective-permute-start | bytes 786440 | tf_op jit(solution)/shard_map/ppermute | solution.py:23
  6.0 8.0 %collective-permute-start.1 = (bf16[32,4096]{1,0:T(8,128)(2,1)}, bf16[32,4096]{1,0:T(8,128)(2,1)S(1)}, u32[]{:S(2)}, u32[]{:S(2)}) collective-permute-start(bf16[32,4096]{1,0:T(8,128)(2,1)} %param.5), channel_id=1, source_target_pairs={{0,1},{1,0},{2,3},{3,2},{4,5},{5,4},{6,7},{7,6},{8,9},{9,8},{10,11... | collective-permute-start | bytes 786440 | tf_op jit(solution)/shard_map/ppermute | solution.py:23
  7.5 8.5 %collective-permute-start.2 = (bf16[32,4096]{1,0:T(8,128)(2,1)}, bf16[32,4096]{1,0:T(8,128)(2,1)S(1)}, u32[]{:S(2)}, u32[]{:S(2)}) collective-permute-start(bf16[32,4096]{1,0:T(8,128)(2,1)} %param.5), channel_id=1, source_target_pairs={{0,2},{1,3},{2,0},{3,1},{4,6},{5,7},{6,4},{7,5},{8,10},{9,11},{10,... | collective-permute-start | bytes 786440 | tf_op jit(solution)/shard_map/ppermute | solution.py:23
  7.5 11.6 %collective-permute-start.3 = (bf16[32,4096]{1,0:T(8,128)(2,1)}, bf16[32,4096]{1,0:T(8,128)(2,1)S(1)}, u32[]{:S(2)}, u32[]{:S(2)}) collective-permute-start(bf16[32,4096]{1,0:T(8,128)(2,1)} %param.5), channel_id=1, source_target_pairs={{0,4},{1,5},{2,6},{3,7},{4,0},{5,1},{6,2},{7,3},{8,12},{9,13},{10,... | collective-permute-start | bytes 786440 | tf_op jit(solution)/shard_map/ppermute | solution.py:23
  14.0 6.9 %collective-permute-start.4 = (bf16[32,4096]{1,0:T(8,128)(2,1)S(1)}, bf16[32,4096]{1,0:T(8,128)(2,1)S(1)}, u32[]{:S(2)}, u32[]{:S(2)}) collective-permute-start(bf16[32,4096]{1,0:T(8,128)(2,1)S(1)} %collective-permute-done), channel_id=1, source_target_pairs={{0,1},{1,0},{2,3},{3,2},{4,5},{5,4},{6,7},{7,6},{8,9},{9,8},{10,11... | collective-permute-start | bytes 786440 | tf_op jit(solution)/shard_map/ppermute | solution.py:23
  15.5 5.3 %collective-permute-start.6 = (bf16[32,4096]{1,0:T(8,128)(2,1)S(1)}, bf16[32,4096]{1,0:T(8,128)(2,1)S(1)}, u32[]{:S(2)}, u32[]{:S(2)}) collective-permute-start(bf16[32,4096]{1,0:T(8,128)(2,1)S(1)} %collective-permute-done), channel_id=1, source_target_pairs={{0,2},{1,3},{2,0},{3,1},{4,6},{5,7},{6,4},{7,5},{8,10},{9,11},{10,... | collective-permute-start | bytes 786440 | tf_op jit(solution)/shard_map/ppermute | solution.py:23
  15.5 5.3 %collective-permute-start.5 = (bf16[32,4096]{1,0:T(8,128)(2,1)S(1)}, bf16[32,4096]{1,0:T(8,128)(2,1)S(1)}, u32[]{:S(2)}, u32[]{:S(2)}) collective-permute-start(bf16[32,4096]{1,0:T(8,128)(2,1)S(1)} %collective-permute-done.1), channel_id=1, source_target_pairs={{0,2},{1,3},{2,0},{3,1},{4,6},{5,7},{6,4},{7,5},{8,10},{9,11},{10,... | collective-permute-start | bytes 786440 | tf_op jit(solution)/shard_map/ppermute | solution.py:23
  16.0 8.2 %collective-permute-start.7 = (bf16[32,4096]{1,0:T(8,128)(2,1)S(1)}, bf16[32,4096]{1,0:T(8,128)(2,1)S(1)}, u32[]{:S(2)}, u32[]{:S(2)}) collective-permute-start(bf16[32,4096]{1,0:T(8,128)(2,1)S(1)} %collective-permute-done.1), channel_id=1, source_target_pairs={{0,4},{1,5},{2,6},{3,7},{4,0},{5,1},{6,2},{7,3},{8,12},{9,13},{10,... | collective-permute-start | bytes 786440 | tf_op jit(solution)/shard_map/ppermute | solution.py:23
  19.1 5.1 %collective-permute-start.8 = (bf16[32,4096]{1,0:T(8,128)(2,1)S(1)}, bf16[32,4096]{1,0:T(8,128)(2,1)S(1)}, u32[]{:S(2)}, u32[]{:S(2)}) collective-permute-start(bf16[32,4096]{1,0:T(8,128)(2,1)S(1)} %collective-permute-done.3), channel_id=1, source_target_pairs={{0,2},{1,3},{2,0},{3,1},{4,6},{5,7},{6,4},{7,5},{8,10},{9,11},{10,... | collective-permute-start | bytes 786440 | tf_op jit(solution)/shard_map/ppermute | solution.py:23
  20.8 3.4 %collective-permute-start.9 = (bf16[32,4096]{1,0:T(8,128)(2,1)S(1)}, bf16[32,4096]{1,0:T(8,128)(2,1)S(1)}, u32[]{:S(2)}, u32[]{:S(2)}) collective-permute-start(bf16[32,4096]{1,0:T(8,128)(2,1)S(1)} %collective-permute-done.4), channel_id=1, source_target_pairs={{0,2},{1,3},{2,0},{3,1},{4,6},{5,7},{6,4},{7,5},{8,10},{9,11},{10,... | collective-permute-start | bytes 786440 | tf_op jit(solution)/shard_map/ppermute | solution.py:23
  24.2 1.5 %collective-permute-start.10 = (bf16[32,4096]{1,0:T(8,128)(2,1)S(1)}, bf16[32,4096]{1,0:T(8,128)(2,1)S(1)}, u32[]{:S(2)}, u32[]{:S(2)}) collective-permute-start(bf16[32,4096]{1,0:T(8,128)(2,1)S(1)} %collective-permute-done.7), channel_id=1, source_target_pairs={{0,2},{1,3},{2,0},{3,1},{4,6},{5,7},{6,4},{7,5},{8,10},{9,11},{10,... | collective-permute-start | bytes 786440 | tf_op jit(solution)/shard_map/ppermute | solution.py:23

commit v2 on v1

--- a/solution.py
+++ b/solution.py
@@ -8,7 +8,7 @@
 from jax.sharding import PartitionSpec as P
 
 AXES = ("body", "row")
-UNROLL = 8
+UNROLL = 16
 SMEM = pl.BlockSpec(memory_space=pltpu.SMEM)
 VMEM = pl.BlockSpec(memory_space=pltpu.VMEM)
 

time: 27.9 us -> 28 us (level)
  waiting for transfers between devices: 6.39 us -> 7.24 us
  Pallas kernels: 11.6 us -> 10.8 us
    pallas_call x3, Pallas kernels: 7.33 us -> 6.44 us  [add_slots(): pl.pallas_call(functools.partial(slots_kernel, stage), out_shape=jax.Shap...]
    ppermute x11, waiting for transfers between devices: 6.39 us -> 7.24 us  [send(): return lax.ppermute(array, AXES, pairs)]
  transfers between devices with their start and end apart: 11 -> 11, of which waited for: 5 -> 5; matrix products, arithmetic and copies ran while one was open for 1% -> 1% of each run, Pallas kernels for 33% -> 30%
where the time goes in v2:
time: 28 us; the launch traced here: 28.1 us
  Pallas kernels  10.8 us (39%)
  starting transfers between devices  9.62 us (34%)
  waiting for transfers between devices  7.24 us (26%)
  other arithmetic  0.36 us (1%)
    ppermute x11, starting transfers between devices, send(): return lax.ppermute(array, AXES, pairs)  9.62 us
    ppermute x11, waiting for transfers between devices, send(): return lax.ppermute(array, AXES, pairs)  7.24 us
    pallas_call x3, Pallas kernels, add_slots(): pl.pallas_call(functools.partial(slots_kernel, stage), out_shape=jax.Shap...  6.44 us
    pallas_call x1, Pallas kernels, prepare(): pl.pallas_call(functools.partial(prepare_kernel, route, stages, row_block...  4.39 us
  transfers between devices with their start and end apart: 11, of which 5 were waited for; matrix products, arithmetic and copies ran while one was open for 1% of the time, Pallas kernels for 30%

profile of v2, /device:TPU:0, one launch (start us, length us, event | category | flops | bytes accessed | tf_op | source)
XLA Modules:
  0.0 28.1 jit_solution(15785230732966056237)
XLA Ops:
  0.0 0.0 copy-start
  0.0 6.0 %collective-permute-start = (bf16[32,4096]{1,0:T(8,128)(2,1)}, bf16[32,4096]{1,0:T(8,128)(2,1)S(1)}, u32[]{:S(2)}, u32[]{:S(2)}) collective-permute-start(bf16[32,4096]{1,0:T(8,128)(2,1)} %param.5), channel_id=1, source_target_pairs={{0,28},{1,29},{2,30},{3,31},{4,8},{5,9},{6,10},{7,11},{8,4},{9,5},... | collective-permute-start | bytes 786440 | tf_op jit(solution)/shard_map/ppermute | solution.py:23
  6.0 1.5 %collective-permute-start.1 = (bf16[32,4096]{1,0:T(8,128)(2,1)}, bf16[32,4096]{1,0:T(8,128)(2,1)S(1)}, u32[]{:S(2)}, u32[]{:S(2)}) collective-permute-start(bf16[32,4096]{1,0:T(8,128)(2,1)} %param.5), channel_id=1, source_target_pairs={{0,1},{1,0},{2,3},{3,2},{4,5},{5,4},{6,7},{7,6},{8,9},{9,8},{10,11... | collective-permute-start | bytes 786440 | tf_op jit(solution)/shard_map/ppermute | solution.py:23
  7.5 0.0 collective-permute-start.2
  7.5 0.0 collective-permute-start.3
  7.5 4.4 %prepare.1 = (bf16[5,32,2,128,128]{4,3,2,1,0:T(8,128)(2,1)S(1)}, s32[3,176]{1,0:T(4,128)S(1)}) custom-call(bf16[1,1,5,32,2,128,128]{6,5,4,3,2,1,0:T(8,128)(2,1)} %infl_ref.1, s32[5,1,32]{2,1,0:T(1,128)} %bitcast.28, s32[5,1,32]{2,1,0:T(1,128)} %bitcast.29, s32[1,1,5]{2,1,0:T(1,128)} %refs_2_.1), custom_call_target="tpu_custom_call" | custom-call | bytes 1024 | tf_op jit(solution)/shard_map/prepare/pallas_call | solution.py:92
  11.9 0.8 %collective-permute-done = bf16[32,4096]{1,0:T(8,128)(2,1)S(1)} collective-permute-done((bf16[32,4096]{1,0:T(8,128)(2,1)}, bf16[32,4096]{1,0:T(8,128)(2,1)S(1)}, u32[]{:S(2)}, u32[]{:S(2)}) %collective-permute-start) | collective-permute-done | bytes 262176 | tf_op jit(solution)/shard_map/ppermute | solution.py:23
  12.7 1.3 %collective-permute-done.1 = bf16[32,4096]{1,0:T(8,128)(2,1)S(1)} collective-permute-done((bf16[32,4096]{1,0:T(8,128)(2,1)}, bf16[32,4096]{1,0:T(8,128)(2,1)S(1)}, u32[]{:S(2)}, u32[]{:S(2)}) %collective-permute-start.1) | collective-permute-done | bytes 262176 | tf_op jit(solution)/shard_map/ppermute | solution.py:23
  14.0 1.5 %collective-permute-start.4 = (bf16[32,4096]{1,0:T(8,128)(2,1)S(1)}, bf16[32,4096]{1,0:T(8,128)(2,1)S(1)}, u32[]{:S(2)}, u32[]{:S(2)}) collective-permute-start(bf16[32,4096]{1,0:T(8,128)(2,1)S(1)} %collective-permute-done), channel_id=1, source_target_pairs={{0,1},{1,0},{2,3},{3,2},{4,5},{5,4},{6,7},{7,6},{8,9},{9,8},{10,11... | collective-permute-start | bytes 786440 | tf_op jit(solution)/shard_map/ppermute | solution.py:23
  15.5 0.0 collective-permute-start.6
  15.5 0.5 %collective-permute-start.5 = (bf16[32,4096]{1,0:T(8,128)(2,1)S(1)}, bf16[32,4096]{1,0:T(8,128)(2,1)S(1)}, u32[]{:S(2)}, u32[]{:S(2)}) collective-permute-start(bf16[32,4096]{1,0:T(8,128)(2,1)S(1)} %collective-permute-done.1), channel_id=1, source_target_pairs={{0,2},{1,3},{2,0},{3,1},{4,6},{5,7},{6,4},{7,5},{8,10},{9,11},{10,... | collective-permute-start | bytes 786440 | tf_op jit(solution)/shard_map/ppermute | solution.py:23
  16.0 0.0 collective-permute-done.2
  16.0 0.0 collective-permute-start.7
  16.0 0.0 copy-done
  16.0 0.1 pad_maximum_fusion.refs_0_
  16.1 2.0 %early_slots.1.refs_0_ = f32[32,4096]{1,0:T(8,128)S(1)} custom-call(bf16[4,32,4096]{2,1,0:T(8,128)(2,1)S(1)} %pad_maximum_fusion.refs_0_, bf16[160,2,128,128]{3,2,1,0:T(8,128)(2,1)S(1)} %bitcast.14, s32[3,176]{1,0:T(4,128)S(1)} %get-tuple-element.18.refs_2_.refs_3_.refs_4_), custom_call_target="tpu_custom_call" | custom-call | bytes 1024 | tf_op jit(solution)/shard_map/early_slots/pallas_call | solution.py:146
  18.2 0.0 collective-permute-done.3
  18.2 0.1 collective-permute-start.8
  18.3 2.5 %collective-permute-done.4 = bf16[32,4096]{1,0:T(8,128)(2,1)S(1)} collective-permute-done((bf16[32,4096]{1,0:T(8,128)(2,1)S(1)}, bf16[32,4096]{1,0:T(8,128)(2,1)S(1)}, u32[]{:S(2)}, u32[]{:S(2)}) %collective-permute-start.4) | collective-permute-done | bytes 262176 | tf_op jit(solution)/shard_map/ppermute | solution.py:23
  20.8 0.0 collective-permute-start.9
  20.8 0.0 collective-permute-done.6
  20.8 0.0 collective-permute-done.5
  20.8 0.1 pad_maximum_fusion.1.refs_1_
  21.0 2.0 %middle_slots.1.refs_0_ = f32[32,4096]{1,0:T(8,128)S(1)} custom-call(f32[32,4096]{1,0:T(8,128)S(1)} %early_slots.1.refs_0_, bf16[4,32,4096]{2,1,0:T(8,128)(2,1)S(1)} %pad_maximum_fusion.1.refs_1_, bf16[160,2,128,128]{3,2,1,0:T(8,128)(2,1)S(1)} %bitcast.15, s32[3,176]{1,0:T(4,128)S(1)} %get-tuple-element.18.refs_2_.refs_3_.refs_4_), custom_call_target="tpu_custom_call" | custom-call | bytes 1024 | tf_op jit(solution)/shard_map/middle_slots/pallas_call | solution.py:146
  23.0 1.2 %collective-permute-done.7 = bf16[32,4096]{1,0:T(8,128)(2,1)S(1)} collective-permute-done((bf16[32,4096]{1,0:T(8,128)(2,1)S(1)}, bf16[32,4096]{1,0:T(8,128)(2,1)S(1)}, u32[]{:S(2)}, u32[]{:S(2)}) %collective-permute-start.7) | collective-permute-done | bytes 262176 | tf_op jit(solution)/shard_map/ppermute | solution.py:23
  24.2 0.0 collective-permute-done.8
  24.2 0.0 collective-permute-done.9
  24.2 0.0 collective-permute-start.10
  24.2 0.1 pad_maximum_fusion.2.refs_2_
  24.3 1.4 %collective-permute-done.10.refs_1_ = bf16[32,4096]{1,0:T(8,128)(2,1)S(1)} collective-permute-done((bf16[32,4096]{1,0:T(8,128)(2,1)S(1)}, bf16[32,4096]{1,0:T(8,128)(2,1)S(1)}, u32[]{:S(2)}, u32[]{:S(2)}) %collective-permute-start.10) | collective-permute-done | bytes 262176 | tf_op jit(solution)/shard_map/ppermute | solution.py:23
  25.8 2.4 %late_slots.1 = f32[32,4096]{1,0:T(8,128)} custom-call(f32[32,4096]{1,0:T(8,128)S(1)} %middle_slots.1.refs_0_, bf16[32,4096]{1,0:T(8,128)(2,1)S(1)} %collective-permute-done.10.refs_1_, bf16[3,32,4096]{2,1,0:T(8,128)(2,1)S(1)} %pad_maximum_fusion.2.refs_2_, bf16[160,2,128,128]{3,2,1,0:T(8,128)(2,1)S(1)} %bitcast.16, ...), custom_call_target="tpu_custom_call" | custom-call | bytes 1024 | tf_op jit(solution)/shard_map/late_slots/pallas_call | solution.py:146
Async XLA Ops:
  0.0 16.0 %copy-start = (bf16[32,4096]{1,0:T(8,128)(2,1)S(1)}, bf16[32,4096]{1,0:T(8,128)(2,1)}, u32[]{:S(2)}) copy-start(bf16[32,4096]{1,0:T(8,128)(2,1)} %param.5) | copy-start | bytes 786436
  0.0 12.7 %collective-permute-start = (bf16[32,4096]{1,0:T(8,128)(2,1)}, bf16[32,4096]{1,0:T(8,128)(2,1)S(1)}, u32[]{:S(2)}, u32[]{:S(2)}) collective-permute-start(bf16[32,4096]{1,0:T(8,128)(2,1)} %param.5), channel_id=1, source_target_pairs={{0,28},{1,29},{2,30},{3,31},{4,8},{5,9},{6,10},{7,11},{8,4},{9,5},... | collective-permute-start | bytes 786440 | tf_op jit(solution)/shard_map/ppermute | solution.py:23
  6.0 8.0 %collective-permute-start.1 = (bf16[32,4096]{1,0:T(8,128)(2,1)}, bf16[32,4096]{1,0:T(8,128)(2,1)S(1)}, u32[]{:S(2)}, u32[]{:S(2)}) collective-permute-start(bf16[32,4096]{1,0:T(8,128)(2,1)} %param.5), channel_id=1, source_target_pairs={{0,1},{1,0},{2,3},{3,2},{4,5},{5,4},{6,7},{7,6},{8,9},{9,8},{10,11... | collective-permute-start | bytes 786440 | tf_op jit(solution)/shard_map/ppermute | solution.py:23
  7.5 8.5 %collective-permute-start.2 = (bf16[32,4096]{1,0:T(8,128)(2,1)}, bf16[32,4096]{1,0:T(8,128)(2,1)S(1)}, u32[]{:S(2)}, u32[]{:S(2)}) collective-permute-start(bf16[32,4096]{1,0:T(8,128)(2,1)} %param.5), channel_id=1, source_target_pairs={{0,2},{1,3},{2,0},{3,1},{4,6},{5,7},{6,4},{7,5},{8,10},{9,11},{10,... | collective-permute-start | bytes 786440 | tf_op jit(solution)/shard_map/ppermute | solution.py:23
  7.5 10.7 %collective-permute-start.3 = (bf16[32,4096]{1,0:T(8,128)(2,1)}, bf16[32,4096]{1,0:T(8,128)(2,1)S(1)}, u32[]{:S(2)}, u32[]{:S(2)}) collective-permute-start(bf16[32,4096]{1,0:T(8,128)(2,1)} %param.5), channel_id=1, source_target_pairs={{0,4},{1,5},{2,6},{3,7},{4,0},{5,1},{6,2},{7,3},{8,12},{9,13},{10,... | collective-permute-start | bytes 786440 | tf_op jit(solution)/shard_map/ppermute | solution.py:23
  14.0 6.9 %collective-permute-start.4 = (bf16[32,4096]{1,0:T(8,128)(2,1)S(1)}, bf16[32,4096]{1,0:T(8,128)(2,1)S(1)}, u32[]{:S(2)}, u32[]{:S(2)}) collective-permute-start(bf16[32,4096]{1,0:T(8,128)(2,1)S(1)} %collective-permute-done), channel_id=1, source_target_pairs={{0,1},{1,0},{2,3},{3,2},{4,5},{5,4},{6,7},{7,6},{8,9},{9,8},{10,11... | collective-permute-start | bytes 786440 | tf_op jit(solution)/shard_map/ppermute | solution.py:23
  15.5 5.3 %collective-permute-start.6 = (bf16[32,4096]{1,0:T(8,128)(2,1)S(1)}, bf16[32,4096]{1,0:T(8,128)(2,1)S(1)}, u32[]{:S(2)}, u32[]{:S(2)}) collective-permute-start(bf16[32,4096]{1,0:T(8,128)(2,1)S(1)} %collective-permute-done), channel_id=1, source_target_pairs={{0,2},{1,3},{2,0},{3,1},{4,6},{5,7},{6,4},{7,5},{8,10},{9,11},{10,... | collective-permute-start | bytes 786440 | tf_op jit(solution)/shard_map/ppermute | solution.py:23
  15.5 5.3 %collective-permute-start.5 = (bf16[32,4096]{1,0:T(8,128)(2,1)S(1)}, bf16[32,4096]{1,0:T(8,128)(2,1)S(1)}, u32[]{:S(2)}, u32[]{:S(2)}) collective-permute-start(bf16[32,4096]{1,0:T(8,128)(2,1)S(1)} %collective-permute-done.1), channel_id=1, source_target_pairs={{0,2},{1,3},{2,0},{3,1},{4,6},{5,7},{6,4},{7,5},{8,10},{9,11},{10,... | collective-permute-start | bytes 786440 | tf_op jit(solution)/shard_map/ppermute | solution.py:23
  16.0 8.2 %collective-permute-start.7 = (bf16[32,4096]{1,0:T(8,128)(2,1)S(1)}, bf16[32,4096]{1,0:T(8,128)(2,1)S(1)}, u32[]{:S(2)}, u32[]{:S(2)}) collective-permute-start(bf16[32,4096]{1,0:T(8,128)(2,1)S(1)} %collective-permute-done.1), channel_id=1, source_target_pairs={{0,4},{1,5},{2,6},{3,7},{4,0},{5,1},{6,2},{7,3},{8,12},{9,13},{10,... | collective-permute-start | bytes 786440 | tf_op jit(solution)/shard_map/ppermute | solution.py:23
  18.2 6.0 %collective-permute-start.8 = (bf16[32,4096]{1,0:T(8,128)(2,1)S(1)}, bf16[32,4096]{1,0:T(8,128)(2,1)S(1)}, u32[]{:S(2)}, u32[]{:S(2)}) collective-permute-start(bf16[32,4096]{1,0:T(8,128)(2,1)S(1)} %collective-permute-done.3), channel_id=1, source_target_pairs={{0,2},{1,3},{2,0},{3,1},{4,6},{5,7},{6,4},{7,5},{8,10},{9,11},{10,... | collective-permute-start | bytes 786440 | tf_op jit(solution)/shard_map/ppermute | solution.py:23
  20.8 3.4 %collective-permute-start.9 = (bf16[32,4096]{1,0:T(8,128)(2,1)S(1)}, bf16[32,4096]{1,0:T(8,128)(2,1)S(1)}, u32[]{:S(2)}, u32[]{:S(2)}) collective-permute-start(bf16[32,4096]{1,0:T(8,128)(2,1)S(1)} %collective-permute-done.4), channel_id=1, source_target_pairs={{0,2},{1,3},{2,0},{3,1},{4,6},{5,7},{6,4},{7,5},{8,10},{9,11},{10,... | collective-permute-start | bytes 786440 | tf_op jit(solution)/shard_map/ppermute | solution.py:23
  24.2 1.5 %collective-permute-start.10 = (bf16[32,4096]{1,0:T(8,128)(2,1)S(1)}, bf16[32,4096]{1,0:T(8,128)(2,1)S(1)}, u32[]{:S(2)}, u32[]{:S(2)}) collective-permute-start(bf16[32,4096]{1,0:T(8,128)(2,1)S(1)} %collective-permute-done.7), channel_id=1, source_target_pairs={{0,2},{1,3},{2,0},{3,1},{4,6},{5,7},{6,4},{7,5},{8,10},{9,11},{10,... | collective-permute-start | bytes 786440 | tf_op jit(solution)/shard_map/ppermute | solution.py:23

commit v3 on v2

--- a/solution.py
+++ b/solution.py
@@ -8,7 +8,7 @@
 from jax.sharding import PartitionSpec as P
 
 AXES = ("body", "row")
-UNROLL = 16
+FETCH, UNROLL = 8, 16
 SMEM = pl.BlockSpec(memory_space=pltpu.SMEM)
 VMEM = pl.BlockSpec(memory_space=pltpu.VMEM)
 
@@ -37,11 +37,11 @@
     sb_copy.start()
 
     def tiles_copy(t, b):
-        span = pl.ds(b * UNROLL, UNROLL)
+        span = pl.ds(b * FETCH, FETCH)
         return pltpu.make_async_copy(infl_ref.at[0, 0, t, span], kept_ref.at[t, span], sems.at[t, b])
 
     def batches(t):
-        return (live_ref[0, 0, t] + (UNROLL - 1)) // UNROLL
+        return (live_ref[0, 0, t] + (FETCH - 1)) // FETCH
 
     for t in range(offsets):
         tiles_copy(t, 0).start()
@@ -58,8 +58,8 @@
 
         def batch(b, counts, t=t, live=live, ways=ways):
             counts = list(counts)
-            for i in range(UNROLL):
-                k = b * UNROLL + i
+            for i in range(FETCH):
+                k = b * FETCH + i
                 sb = sb_ref[t, 0, k]
                 block, (stage, piece) = sb, ways[0]
                 for s in range(1, len(ways)):
@@ -101,7 +101,7 @@
             pltpu.SMEM((offsets, 1, capacity), jnp.int32),
             pltpu.SMEM((offsets, 1, capacity), jnp.int32),
             pltpu.SMEM(live_counts.shape, jnp.int32),
-            pltpu.SemaphoreType.DMA((offsets, capacity // UNROLL)),
+            pltpu.SemaphoreType.DMA((offsets, capacity // FETCH)),
             pltpu.SemaphoreType.DMA((3,)),
         ],
         compiler_params=pltpu.CompilerParams(vmem_limit_bytes=4 << 20),

time: 28 us -> 28.3 us (1.011)
  starting transfers between devices: 9.62 us -> 10.1 us
  Pallas kernels: 10.8 us -> 11.1 us
    pallas_call x3, Pallas kernels: 6.44 us -> 6.92 us  [add_slots(): pl.pallas_call(functools.partial(slots_kernel, stage), out_shape=jax.Shap...]
    ppermute x11, starting transfers between devices: 9.62 us -> 10.1 us  [send(): return lax.ppermute(array, AXES, pairs)]
  transfers between devices with their start and end apart: 11 -> 11, of which waited for: 5 -> 5; matrix products, arithmetic and copies ran while one was open for 1% -> 1% of each run, Pallas kernels for 30% -> 29%
where the time goes in v3:
time: 28.3 us; the launch traced here: 28.6 us
  Pallas kernels  11.1 us (39%)
  starting transfers between devices  10.1 us (36%)
  waiting for transfers between devices  7.01 us (25%)
  other arithmetic  0.36 us (1%)
    ppermute x11, starting transfers between devices, send(): return lax.ppermute(array, AXES, pairs)  10.1 us
    ppermute x11, waiting for transfers between devices, send(): return lax.ppermute(array, AXES, pairs)  7.01 us
    pallas_call x3, Pallas kernels, add_slots(): pl.pallas_call(functools.partial(slots_kernel, stage), out_shape=jax.Shap...  6.92 us
    pallas_call x1, Pallas kernels, prepare(): pl.pallas_call(functools.partial(prepare_kernel, route, stages, row_block...  4.15 us
  transfers between devices with their start and end apart: 11, of which 5 were waited for; matrix products, arithmetic and copies ran while one was open for 1% of the time, Pallas kernels for 29%

profile of v3, /device:TPU:0, one launch (start us, length us, event | category | flops | bytes accessed | tf_op | source)
XLA Modules:
  0.0 28.6 jit_solution(13199998438766871027)
XLA Ops:
  0.0 0.0 copy-start
  0.0 6.0 %collective-permute-start = (bf16[32,4096]{1,0:T(8,128)(2,1)}, bf16[32,4096]{1,0:T(8,128)(2,1)S(1)}, u32[]{:S(2)}, u32[]{:S(2)}) collective-permute-start(bf16[32,4096]{1,0:T(8,128)(2,1)} %param.5), channel_id=1, source_target_pairs={{0,28},{1,29},{2,30},{3,31},{4,8},{5,9},{6,10},{7,11},{8,4},{9,5},... | collective-permute-start | bytes 786440 | tf_op jit(solution)/shard_map/ppermute | solution.py:23
  6.0 1.5 %collective-permute-start.1 = (bf16[32,4096]{1,0:T(8,128)(2,1)}, bf16[32,4096]{1,0:T(8,128)(2,1)S(1)}, u32[]{:S(2)}, u32[]{:S(2)}) collective-permute-start(bf16[32,4096]{1,0:T(8,128)(2,1)} %param.5), channel_id=1, source_target_pairs={{0,1},{1,0},{2,3},{3,2},{4,5},{5,4},{6,7},{7,6},{8,9},{9,8},{10,11... | collective-permute-start | bytes 786440 | tf_op jit(solution)/shard_map/ppermute | solution.py:23
  7.5 0.0 collective-permute-start.2
  7.5 0.0 collective-permute-start.3
  7.5 4.1 %prepare.1 = (bf16[5,32,2,128,128]{4,3,2,1,0:T(8,128)(2,1)S(1)}, s32[3,176]{1,0:T(4,128)S(1)}) custom-call(bf16[1,1,5,32,2,128,128]{6,5,4,3,2,1,0:T(8,128)(2,1)} %infl_ref.1, s32[5,1,32]{2,1,0:T(1,128)} %bitcast.28, s32[5,1,32]{2,1,0:T(1,128)} %bitcast.29, s32[1,1,5]{2,1,0:T(1,128)} %refs_2_.1), custom_call_target="tpu_custom_call" | custom-call | bytes 1024 | tf_op jit(solution)/shard_map/prepare/pallas_call | solution.py:92
  11.7 1.0 %collective-permute-done = bf16[32,4096]{1,0:T(8,128)(2,1)S(1)} collective-permute-done((bf16[32,4096]{1,0:T(8,128)(2,1)}, bf16[32,4096]{1,0:T(8,128)(2,1)S(1)}, u32[]{:S(2)}, u32[]{:S(2)}) %collective-permute-start) | collective-permute-done | bytes 262176 | tf_op jit(solution)/shard_map/ppermute | solution.py:23
  12.7 1.3 %collective-permute-done.1 = bf16[32,4096]{1,0:T(8,128)(2,1)S(1)} collective-permute-done((bf16[32,4096]{1,0:T(8,128)(2,1)}, bf16[32,4096]{1,0:T(8,128)(2,1)S(1)}, u32[]{:S(2)}, u32[]{:S(2)}) %collective-permute-start.1) | collective-permute-done | bytes 262176 | tf_op jit(solution)/shard_map/ppermute | solution.py:23
  14.0 1.5 %collective-permute-start.4 = (bf16[32,4096]{1,0:T(8,128)(2,1)S(1)}, bf16[32,4096]{1,0:T(8,128)(2,1)S(1)}, u32[]{:S(2)}, u32[]{:S(2)}) collective-permute-start(bf16[32,4096]{1,0:T(8,128)(2,1)S(1)} %collective-permute-done), channel_id=1, source_target_pairs={{0,1},{1,0},{2,3},{3,2},{4,5},{5,4},{6,7},{7,6},{8,9},{9,8},{10,11... | collective-permute-start | bytes 786440 | tf_op jit(solution)/shard_map/ppermute | solution.py:23
  15.5 0.0 collective-permute-start.6
  15.5 0.5 %collective-permute-start.5 = (bf16[32,4096]{1,0:T(8,128)(2,1)S(1)}, bf16[32,4096]{1,0:T(8,128)(2,1)S(1)}, u32[]{:S(2)}, u32[]{:S(2)}) collective-permute-start(bf16[32,4096]{1,0:T(8,128)(2,1)S(1)} %collective-permute-done.1), channel_id=1, source_target_pairs={{0,2},{1,3},{2,0},{3,1},{4,6},{5,7},{6,4},{7,5},{8,10},{9,11},{10,... | collective-permute-start | bytes 786440 | tf_op jit(solution)/shard_map/ppermute | solution.py:23
  16.0 0.0 collective-permute-done.2
  16.0 0.0 collective-permute-start.7
  16.0 0.0 copy-done
  16.0 0.1 pad_maximum_fusion.refs_0_
  16.1 2.0 %early_slots.1.refs_0_ = f32[32,4096]{1,0:T(8,128)S(1)} custom-call(bf16[4,32,4096]{2,1,0:T(8,128)(2,1)S(1)} %pad_maximum_fusion.refs_0_, bf16[160,2,128,128]{3,2,1,0:T(8,128)(2,1)S(1)} %bitcast.14, s32[3,176]{1,0:T(4,128)S(1)} %get-tuple-element.18.refs_2_.refs_3_.refs_4_), custom_call_target="tpu_custom_call" | custom-call | bytes 1024 | tf_op jit(solution)/shard_map/early_slots/pallas_call | solution.py:146
  18.2 0.0 collective-permute-done.3
  18.2 0.5 %collective-permute-start.8 = (bf16[32,4096]{1,0:T(8,128)(2,1)S(1)}, bf16[32,4096]{1,0:T(8,128)(2,1)S(1)}, u32[]{:S(2)}, u32[]{:S(2)}) collective-permute-start(bf16[32,4096]{1,0:T(8,128)(2,1)S(1)} %collective-permute-done.3), channel_id=1, source_target_pairs={{0,2},{1,3},{2,0},{3,1},{4,6},{5,7},{6,4},{7,5},{8,10},{9,11},{10,... | collective-permute-start | bytes 786440 | tf_op jit(solution)/shard_map/ppermute | solution.py:23
  18.7 2.3 %collective-permute-done.4 = bf16[32,4096]{1,0:T(8,128)(2,1)S(1)} collective-permute-done((bf16[32,4096]{1,0:T(8,128)(2,1)S(1)}, bf16[32,4096]{1,0:T(8,128)(2,1)S(1)}, u32[]{:S(2)}, u32[]{:S(2)}) %collective-permute-start.4) | collective-permute-done | bytes 262176 | tf_op jit(solution)/shard_map/ppermute | solution.py:23
  21.0 0.0 collective-permute-start.9
  21.0 0.0 collective-permute-done.6
  21.0 0.0 collective-permute-done.5
  21.1 0.1 pad_maximum_fusion.1.refs_1_
  21.2 2.0 %middle_slots.1.refs_0_ = f32[32,4096]{1,0:T(8,128)S(1)} custom-call(f32[32,4096]{1,0:T(8,128)S(1)} %early_slots.1.refs_0_, bf16[4,32,4096]{2,1,0:T(8,128)(2,1)S(1)} %pad_maximum_fusion.1.refs_1_, bf16[160,2,128,128]{3,2,1,0:T(8,128)(2,1)S(1)} %bitcast.15, s32[3,176]{1,0:T(4,128)S(1)} %get-tuple-element.18.refs_2_.refs_3_.refs_4_), custom_call_target="tpu_custom_call" | custom-call | bytes 1024 | tf_op jit(solution)/shard_map/middle_slots/pallas_call | solution.py:146
  23.2 1.0 %collective-permute-done.7 = bf16[32,4096]{1,0:T(8,128)(2,1)S(1)} collective-permute-done((bf16[32,4096]{1,0:T(8,128)(2,1)S(1)}, bf16[32,4096]{1,0:T(8,128)(2,1)S(1)}, u32[]{:S(2)}, u32[]{:S(2)}) %collective-permute-start.7) | collective-permute-done | bytes 262176 | tf_op jit(solution)/shard_map/ppermute | solution.py:23
  24.2 0.0 collective-permute-done.8
  24.2 0.0 collective-permute-done.9
  24.2 0.0 collective-permute-start.10
  24.2 0.1 pad_maximum_fusion.2.refs_2_
  24.3 1.4 %collective-permute-done.10.refs_1_ = bf16[32,4096]{1,0:T(8,128)(2,1)S(1)} collective-permute-done((bf16[32,4096]{1,0:T(8,128)(2,1)S(1)}, bf16[32,4096]{1,0:T(8,128)(2,1)S(1)}, u32[]{:S(2)}, u32[]{:S(2)}) %collective-permute-start.10) | collective-permute-done | bytes 262176 | tf_op jit(solution)/shard_map/ppermute | solution.py:23
  25.8 2.8 %late_slots.1 = f32[32,4096]{1,0:T(8,128)} custom-call(f32[32,4096]{1,0:T(8,128)S(1)} %middle_slots.1.refs_0_, bf16[32,4096]{1,0:T(8,128)(2,1)S(1)} %collective-permute-done.10.refs_1_, bf16[3,32,4096]{2,1,0:T(8,128)(2,1)S(1)} %pad_maximum_fusion.2.refs_2_, bf16[160,2,128,128]{3,2,1,0:T(8,128)(2,1)S(1)} %bitcast.16, ...), custom_call_target="tpu_custom_call" | custom-call | bytes 1024 | tf_op jit(solution)/shard_map/late_slots/pallas_call | solution.py:146
Async XLA Ops:
  0.0 16.0 %copy-start = (bf16[32,4096]{1,0:T(8,128)(2,1)S(1)}, bf16[32,4096]{1,0:T(8,128)(2,1)}, u32[]{:S(2)}) copy-start(bf16[32,4096]{1,0:T(8,128)(2,1)} %param.5) | copy-start | bytes 786436
  0.0 12.7 %collective-permute-start = (bf16[32,4096]{1,0:T(8,128)(2,1)}, bf16[32,4096]{1,0:T(8,128)(2,1)S(1)}, u32[]{:S(2)}, u32[]{:S(2)}) collective-permute-start(bf16[32,4096]{1,0:T(8,128)(2,1)} %param.5), channel_id=1, source_target_pairs={{0,28},{1,29},{2,30},{3,31},{4,8},{5,9},{6,10},{7,11},{8,4},{9,5},... | collective-permute-start | bytes 786440 | tf_op jit(solution)/shard_map/ppermute | solution.py:23
  6.0 8.0 %collective-permute-start.1 = (bf16[32,4096]{1,0:T(8,128)(2,1)}, bf16[32,4096]{1,0:T(8,128)(2,1)S(1)}, u32[]{:S(2)}, u32[]{:S(2)}) collective-permute-start(bf16[32,4096]{1,0:T(8,128)(2,1)} %param.5), channel_id=1, source_target_pairs={{0,1},{1,0},{2,3},{3,2},{4,5},{5,4},{6,7},{7,6},{8,9},{9,8},{10,11... | collective-permute-start | bytes 786440 | tf_op jit(solution)/shard_map/ppermute | solution.py:23
  7.5 8.5 %collective-permute-start.2 = (bf16[32,4096]{1,0:T(8,128)(2,1)}, bf16[32,4096]{1,0:T(8,128)(2,1)S(1)}, u32[]{:S(2)}, u32[]{:S(2)}) collective-permute-start(bf16[32,4096]{1,0:T(8,128)(2,1)} %param.5), channel_id=1, source_target_pairs={{0,2},{1,3},{2,0},{3,1},{4,6},{5,7},{6,4},{7,5},{8,10},{9,11},{10,... | collective-permute-start | bytes 786440 | tf_op jit(solution)/shard_map/ppermute | solution.py:23
  7.5 10.7 %collective-permute-start.3 = (bf16[32,4096]{1,0:T(8,128)(2,1)}, bf16[32,4096]{1,0:T(8,128)(2,1)S(1)}, u32[]{:S(2)}, u32[]{:S(2)}) collective-permute-start(bf16[32,4096]{1,0:T(8,128)(2,1)} %param.5), channel_id=1, source_target_pairs={{0,4},{1,5},{2,6},{3,7},{4,0},{5,1},{6,2},{7,3},{8,12},{9,13},{10,... | collective-permute-start | bytes 786440 | tf_op jit(solution)/shard_map/ppermute | solution.py:23
  14.0 7.1 %collective-permute-start.4 = (bf16[32,4096]{1,0:T(8,128)(2,1)S(1)}, bf16[32,4096]{1,0:T(8,128)(2,1)S(1)}, u32[]{:S(2)}, u32[]{:S(2)}) collective-permute-start(bf16[32,4096]{1,0:T(8,128)(2,1)S(1)} %collective-permute-done), channel_id=1, source_target_pairs={{0,1},{1,0},{2,3},{3,2},{4,5},{5,4},{6,7},{7,6},{8,9},{9,8},{10,11... | collective-permute-start | bytes 786440 | tf_op jit(solution)/shard_map/ppermute | solution.py:23
  15.5 5.6 %collective-permute-start.6 = (bf16[32,4096]{1,0:T(8,128)(2,1)S(1)}, bf16[32,4096]{1,0:T(8,128)(2,1)S(1)}, u32[]{:S(2)}, u32[]{:S(2)}) collective-permute-start(bf16[32,4096]{1,0:T(8,128)(2,1)S(1)} %collective-permute-done), channel_id=1, source_target_pairs={{0,2},{1,3},{2,0},{3,1},{4,6},{5,7},{6,4},{7,5},{8,10},{9,11},{10,... | collective-permute-start | bytes 786440 | tf_op jit(solution)/shard_map/ppermute | solution.py:23
  15.5 5.6 %collective-permute-start.5 = (bf16[32,4096]{1,0:T(8,128)(2,1)S(1)}, bf16[32,4096]{1,0:T(8,128)(2,1)S(1)}, u32[]{:S(2)}, u32[]{:S(2)}) collective-permute-start(bf16[32,4096]{1,0:T(8,128)(2,1)S(1)} %collective-permute-done.1), channel_id=1, source_target_pairs={{0,2},{1,3},{2,0},{3,1},{4,6},{5,7},{6,4},{7,5},{8,10},{9,11},{10,... | collective-permute-start | bytes 786440 | tf_op jit(solution)/shard_map/ppermute | solution.py:23
  16.0 8.2 %collective-permute-start.7 = (bf16[32,4096]{1,0:T(8,128)(2,1)S(1)}, bf16[32,4096]{1,0:T(8,128)(2,1)S(1)}, u32[]{:S(2)}, u32[]{:S(2)}) collective-permute-start(bf16[32,4096]{1,0:T(8,128)(2,1)S(1)} %collective-permute-done.1), channel_id=1, source_target_pairs={{0,4},{1,5},{2,6},{3,7},{4,0},{5,1},{6,2},{7,3},{8,12},{9,13},{10,... | collective-permute-start | bytes 786440 | tf_op jit(solution)/shard_map/ppermute | solution.py:23
  18.2 6.0 %collective-permute-start.8 = (bf16[32,4096]{1,0:T(8,128)(2,1)S(1)}, bf16[32,4096]{1,0:T(8,128)(2,1)S(1)}, u32[]{:S(2)}, u32[]{:S(2)}) collective-permute-start(bf16[32,4096]{1,0:T(8,128)(2,1)S(1)} %collective-permute-done.3), channel_id=1, source_target_pairs={{0,2},{1,3},{2,0},{3,1},{4,6},{5,7},{6,4},{7,5},{8,10},{9,11},{10,... | collective-permute-start | bytes 786440 | tf_op jit(solution)/shard_map/ppermute | solution.py:23
  21.0 3.2 %collective-permute-start.9 = (bf16[32,4096]{1,0:T(8,128)(2,1)S(1)}, bf16[32,4096]{1,0:T(8,128)(2,1)S(1)}, u32[]{:S(2)}, u32[]{:S(2)}) collective-permute-start(bf16[32,4096]{1,0:T(8,128)(2,1)S(1)} %collective-permute-done.4), channel_id=1, source_target_pairs={{0,2},{1,3},{2,0},{3,1},{4,6},{5,7},{6,4},{7,5},{8,10},{9,11},{10,... | collective-permute-start | bytes 786440 | tf_op jit(solution)/shard_map/ppermute | solution.py:23
  24.2 1.5 %collective-permute-start.10 = (bf16[32,4096]{1,0:T(8,128)(2,1)S(1)}, bf16[32,4096]{1,0:T(8,128)(2,1)S(1)}, u32[]{:S(2)}, u32[]{:S(2)}) collective-permute-start(bf16[32,4096]{1,0:T(8,128)(2,1)S(1)} %collective-permute-done.7), channel_id=1, source_target_pairs={{0,2},{1,3},{2,0},{3,1},{4,6},{5,7},{6,4},{7,5},{8,10},{9,11},{10,... | collective-permute-start | bytes 786440 | tf_op jit(solution)/shard_map/ppermute | solution.py:23
